TPU v7x, 32 devices: a whole 2x2x4 slice. The times are simulated.
32 devices in a mesh: row: 4 (over z), phi: 8 (over y, x, core).
Axes of the slice: x: 2, y: 2, z: 4, core: 2. Of those that a mesh axis runs over, the one named last changes fastest.
Arguments:
- fields: float32 [5, 64, 64, 4096], P(None, 'row', None, 'phi'), may hold values from -6 to 6
- offsets: int32 [64], P('row'), may hold values from 0 to 4095
- fraction: float32 [64], P('row'), may hold values from 0 to 1
- radial_diff: float32 [64], P('row'), may hold values from 0.05 to 0.15
- radial_drift: float32 [64], P('row'), may hold values from -0.05 to 0.05
- loop_diff: float32 [64], P('row'), may hold values from 0.05 to 0.15
- height_diff: float32 [64], replicated, may hold values from 0.05 to 0.15
Outputs:
- evolved: float32 [5, 64, 64, 4096], P(None, 'row', None, 'phi')
All inputs are finite; a program needn't handle non-finite values.
Results may differ from a plain program's by a relative error of at most 0.00002.
Values sent between devices are 32-bit elements; how exact they have to be, the bound alone decides.
A program may use at most 128 MiB of HBM per device.

v0:
```python
import jax
import jax.numpy as jnp
from jax import lax
from jax.sharding import PartitionSpec as P

HYDRO = 2


def with_halo(cells, sides, width, closed):
    for axis, dim in sides:
        count = lax.axis_size(axis)
        ends = count if closed else count - 1
        head = lax.slice_in_dim(cells, 0, width, axis=dim)
        tail = lax.slice_in_dim(cells, cells.shape[dim] - width, cells.shape[dim], axis=dim)
        cells = jnp.concatenate(
            [
                lax.ppermute(tail, axis, [(i, (i + 1) % count) for i in range(ends)]),
                cells,
                lax.ppermute(head, axis, [((i + 1) % count, i) for i in range(ends)]),
            ],
            axis=dim,
        )
    return cells


def combine(
    state, upper, lower, east, west, above, below, radial_diff, radial_drift, loop_diff, height_diff
):
    w_rad = radial_diff[None, :, None, None]
    v_rad = radial_drift[None, :, None, None]
    a_loop = loop_diff[None, :, None, None]
    c_height = height_diff[None, None, :, None]
    result = state + w_rad * (upper - 2.0 * state + lower) + v_rad * (upper - lower)
    result = result + a_loop * (east - 2.0 * state + west)
    return result + c_height * (above - 2.0 * state + below)


def barrel_shift(values, amounts, limit):
    bit_count = max(limit - 1, 1).bit_length()
    for level in range(bit_count):
        step_size = 1 << level
        rolled = jnp.roll(values, step_size, axis=3)
        taken = amounts >> level & 1 == 1
        values = jnp.where(taken[None, :, None, None], rolled, values)
    return values


def local(fields, offsets, fraction, radial_diff, radial_drift, loop_diff, height_diff):
    loops = lax.all_to_all(fields, "phi", split_axis=1, concat_axis=3, tiled=True)
    count = loops.shape[1]
    loop_cells = loops.shape[3]
    start = lax.axis_index("phi") * count
    my_offsets = lax.dynamic_slice_in_dim(offsets, start, count)
    my_fraction = lax.dynamic_slice_in_dim(fraction, start, count)
    part_one = barrel_shift(loops, my_offsets, loop_cells)
    part_two = jnp.roll(part_one, 1, axis=3)
    weight = my_fraction[None, :, None, None]
    shifted_loops = (1.0 - weight) * part_one + weight * part_two
    state = lax.all_to_all(shifted_loops, "phi", split_axis=3, concat_axis=1, tiled=True)
    for substep in range(HYDRO):
        radial_pad = with_halo(state, (("row", 1),), 1, False)
        loop_pad = with_halo(state, (("phi", 3),), 1, True)
        height_pad = jnp.pad(state, ((0, 0), (0, 0), (1, 1), (0, 0)))
        state = combine(
            state,
            radial_pad[:, 2:],
            radial_pad[:, :-2],
            loop_pad[:, :, :, 2:],
            loop_pad[:, :, :, :-2],
            height_pad[:, :, 2:],
            height_pad[:, :, :-2],
            radial_diff,
            radial_drift,
            loop_diff,
            height_diff,
        )
    return state


def solution(mesh):
    placed = (P(None, "row", None, "phi"), P("row"), P("row"), P("row"), P("row"), P("row"), P())
    return jax.shard_map(
        local, mesh=mesh, in_specs=placed, out_specs=P(None, "row", None, "phi"), check_vma=False
    )
```

profile of v0, /device:TPU:0, one launch (start us, length us, event | category | flops | bytes accessed | tf_op | source)
XLA Modules:
  0.0 643.2 jit_solution(6712182637961851663)
XLA Ops:
  0.0 10.4 %copy.11 = f32[5,16,64,512]{3,2,0,1:T(8,128)} copy(f32[5,16,64,512]{3,2,1,0:T(8,128)} %param.7) | data formatting | bytes 20971520 | tf_op args[0]
  10.4 5.3 all-to-all-start
  15.9 117.0 %all-to-all-done = f32[5,16,64,512]{3,2,0,1:T(8,128)} async-done(((f32[5,16,64,512]{3,2,0,1:T(8,128)}), f32[5,16,64,512]{3,2,0,1:T(8,128)}, u32[]{:S(2)}, u32[]{:S(2)}) %all-to-all-start) | async-done | bytes 10485792 | tf_op jit(solution)/shard_map/all_to_all | solution.py:49
  132.9 14.8 %copy.27 = f32[5,8,2,64,512]{4,1,3,2,0:T(8,128)} copy(f32[5,8,2,64,512]{4,3,0,2,1:T(8,128)} %bitcast) | data formatting | bytes 20971520 | tf_op jit(solution)/shard_map/all_to_all | solution.py:49
  147.7 11.6 %all_to_all.29 = f32[5,2,64,4096]{3,2,1,0:T(8,128)} reshape(f32[5,2,64,8,512]{4,3,2,1,0:T(8,128)} %bitcast.34) | data formatting | bytes 20971520 | tf_op jit(solution)/shard_map/all_to_all | solution.py:49
  159.3 1.1 slice.216
  160.5 8.6 %maximum_select_fusion = f32[5,2,64,4096]{3,2,1,0:T(8,128)S(1)} fusion(f32[5,2,64,4096]{3,2,1,0:T(8,128)} %all_to_all.29, f32[5,2,64,4095]{3,2,1,0:T(8,128)} %bitcast.28, f32[5,2,64,1]{3,2,1,0:T(8,128)S(1)} %slice.216, pred[2]{0:T(512)(128)(4,1)S(1)} %get-tuple-element.29), kind=kLoop, calls=%fused_computation.42 | loop fusion | flops 5242880 | bytes 31457282 | tf_op jit(solution)/shard_map/jit(_where)/select_n | solution.py:44
  169.0 0.2 slice.218
  169.2 2.9 maximum_select_fusion.1
  172.1 0.2 slice.220
  172.3 3.1 maximum_select_fusion.2
  175.4 0.2 slice.222
  175.5 2.9 maximum_select_fusion.3
  178.4 0.2 slice.224
  178.6 2.9 maximum_select_fusion.4
  181.7 2.9 maximum_select_fusion.5
  184.7 2.9 maximum_select_fusion.6
  187.7 5.1 slice.231
  192.8 2.0 copy-done.2
  194.8 7.8 %maximum_select_fusion.7 = f32[5,2,64,4096]{3,2,1,0:T(8,128)S(1)} fusion(f32[5,2,64,4096]{3,2,1,0:T(8,128)} %copy-done.2, f32[5,2,64,3968]{3,2,1,0:T(8,128)} %slice.231, f32[5,2,64,128]{3,2,1,0:T(8,128)S(1)} %slice.230, pred[2]{0:T(512)(128)(4,1)S(1)} %get-tuple-element.26), kind=kLoop, calls=%fused_computation.49 | loop fusion | flops 5242880 | bytes 31457282 | tf_op jit(solution)/shard_map/jit(_where)/select_n | solution.py:44
  202.6 4.6 slice.233
  207.2 9.3 %maximum_select_fusion.8 = f32[5,2,64,4096]{3,2,1,0:T(8,128)} fusion(f32[5,2,64,4096]{3,2,1,0:T(8,128)S(1)} %maximum_select_fusion.7, f32[5,2,64,3840]{3,2,1,0:T(8,128)} %slice.233, f32[5,2,64,256]{3,2,1,0:T(8,128)S(1)} %slice.232, pred[2]{0:T(512)(128)(4,1)S(1)} %get-tuple-element.27), kind=kLoop, calls=%fused_computation.50 | loop fusion | flops 5242880 | bytes 31457282 | tf_op jit(solution)/shard_map/jit(_where)/select_n | solution.py:44
  216.5 3.6 slice-done
  220.1 0.3 slice-done.1
  220.5 4.9 maximum_select_fusion.9
  225.4 4.4 slice.237
  229.8 0.2 slice.236
  230.0 1.9 copy-done.1
  231.9 7.5 %maximum_select_fusion.10 = f32[5,2,64,4096]{3,2,1,0:T(8,128)S(1)} fusion(f32[5,2,64,4096]{3,2,1,0:T(8,128)} %copy-done.1, f32[5,2,64,3072]{3,2,1,0:T(8,128)} %slice.237, f32[5,2,64,1024]{3,2,1,0:T(8,128)S(1)} %slice.236, pred[2]{0:T(512)(128)(4,1)S(1)} %get-tuple-element.19), kind=kLoop, calls=%fused_computation.52 | loop fusion | flops 5242880 | bytes 31457282 | tf_op jit(solution)/shard_map/jit(_where)/select_n | solution.py:44
  239.4 5.3 fusion.33
  244.6 2.0 copy-done
  246.6 7.8 %maximum_select_fusion.11 = f32[5,2,64,4096]{3,2,1,0:T(8,128)S(1)} fusion(f32[5,2,64,4096]{3,2,1,0:T(8,128)} %copy-done, f32[5,2,64,2048]{3,2,1,0:T(8,128)} %get-tuple-element.18, f32[5,2,64,2048]{3,2,1,0:T(8,128)} %get-tuple-element.17, pred[2]{0:T(512)(128)(4,1)S(1)} %get-tuple-element.7), kind=kLoop, calls=%fused_computation.53 | loop fusion | flops 5242880 | bytes 31457282 | tf_op jit(solution)/shard_map/jit(_where)/select_n | solution.py:44
  254.6 5.5 fusion.28
  260.1 24.8 %copy.13 = f32[5,2,64,4096]{2,1,0,3:T(2,128)} copy(f32[5,2,64,4096]{3,2,1,0:T(8,128)} %fusion.28) | data formatting | bytes 20971520 | tf_op jit(solution)/shard_map/add | solution.py:58
  284.9 24.7 %reshape.19 = f32[8,1,327680]{2,1,0:T(1,128)} reshape(f32[4096,5,2,64]{3,2,1,0:T(2,128)} %bitcast.29) | data formatting | bytes 20971520
  309.6 122.5 %all_to_all.36 = f32[8,1,327680]{2,1,0:T(1,128)} all-to-all(f32[8,1,327680]{2,1,0:T(1,128)} %reshape.19), channel_id=1, replica_groups=mesh['row'=4,'phi'=8] {'phi'}, dimensions={0} | all-to-all | bytes 20971520 | tf_op jit(solution)/shard_map/all_to_all | solution.py:59
  432.2 0.5 broadcast.105
  432.7 31.3 %reduce = f32[8,327680]{1,0:T(8,128)} reduce(f32[8,1,327680]{2,1,0:T(1,128)} %all_to_all.36, f32[]{:T(128)} %broadcast.105), dimensions={1}, to_apply=%all_to_all.30.reduce_sub_computation | reduce | bytes 20971524 | tf_op jit(solution)/shard_map/all_to_all | solution.py:59
  464.0 37.3 %reshape.20 = f32[4096,5,2,64]{3,2,1,0:T(2,128)} reshape(f32[8,327680]{1,0:T(8,128)} %reduce) | data formatting | bytes 20971520
  501.3 24.9 %copy.25 = f32[5,2,64,8,512]{4,2,1,3,0:T(8,128)} copy(f32[5,2,64,8,512]{2,1,0,4,3:T(2,128)} %bitcast.30) | data formatting | bytes 20971520 | tf_op jit(solution)/shard_map/all_to_all | solution.py:59
  526.2 2.5 fusion.31
  528.7 1.3 collective-permute-start
  530.0 5.9 collective-permute-start.1
  535.9 5.1 fusion.32
  541.0 2.6 copy.16
  543.7 0.8 copy.18
  544.5 0.5 collective-permute-start.3
  545.0 0.3 collective-permute-done.2
  545.3 0.8 copy.17
  546.2 2.7 collective-permute-done.3
  548.8 2.4 copy.19
  551.2 34.3 %fusion.3 = f32[5,16,64,512]{3,2,1,0:T(8,128)S(1)} fusion(f32[5,16,64,512]{3,2,1,0:T(8,128)} %bitcast.33, f32[5,16,64,1]{3,2,1,0:T(8,128)} %copy.19, f32[5,16,64,1]{3,2,1,0:T(8,128)S(1)} %copy.17, f32[5,1,64,512]{3,2,1,0:T(8,128)} %collective-permute-done.1, f32[5,1,64,512]{3,2,1,0:T(8,128)S(1)} %collective-permute-done, f32[64]{0:T(128)S(1)} %copy-done.4, ...), kind=kLoop, calls=%fused_computation.7 | loop fusion | flops 52428800 | bytes 22323648 | tf_op jit(solution)/shard_map/add | solution.py:35
  585.6 1.3 fusion.29
  586.9 1.3 collective-permute-start.4
  588.1 5.6 collective-permute-start.5
  593.8 2.5 fusion.30
  596.3 2.6 copy.20
  598.9 0.8 copy.22
  599.8 0.5 collective-permute-start.7
  600.3 0.3 collective-permute-done.6
  600.6 0.8 copy.21
  601.4 2.7 collective-permute-done.7
  604.1 2.4 copy.23
  606.5 36.3 %fusion.7 = f32[5,16,64,512]{3,2,1,0:T(8,128)} fusion(f32[5,16,64,512]{3,2,1,0:T(8,128)} %copy-done.3, f32[5,16,64,1]{3,2,1,0:T(8,128)} %copy.23, f32[5,16,64,1]{3,2,1,0:T(8,128)S(1)} %copy.21, f32[5,1,64,512]{3,2,1,0:T(8,128)} %collective-permute-done.5, f32[5,1,64,512]{3,2,1,0:T(8,128)S(1)} %collective-permute-done.4, f32[64]{0:T(128)S(1)} %copy-done.4, ...), kind=kLoop, calls=%fused_computation.11 | loop fusion | flops 52428800 | bytes 22323648 | tf_op jit(solution)/shard_map/add | solution.py:35
  (33 shorter events, 0.9 us)
Async XLA Ops:
  10.4 5.3 copy-start.8
  10.4 5.4 copy-start.9
  10.4 122.5 %all-to-all-start = ((f32[5,16,64,512]{3,2,0,1:T(8,128)}), f32[5,16,64,512]{3,2,0,1:T(8,128)}, u32[]{:S(2)}, u32[]{:S(2)}) async-start(f32[5,16,64,512]{3,2,0,1:T(8,128)} %copy.11), calls=%async_computation | async-start | bytes 20971520 | tf_op jit(solution)/shard_map/all_to_all | solution.py:49
  187.6 7.1 %copy-start.2 = (f32[5,2,64,4096]{3,2,1,0:T(8,128)}, f32[5,2,64,4096]{3,2,1,0:T(8,128)S(1)}, u32[]{:S(2)}) copy-start(f32[5,2,64,4096]{3,2,1,0:T(8,128)S(1)} %maximum_select_fusion.6) | copy-start | bytes 31457284
  216.5 3.6 slice-start
  216.5 3.9 slice-start.1
  225.4 6.5 %copy-start.1 = (f32[5,2,64,4096]{3,2,1,0:T(8,128)}, f32[5,2,64,4096]{3,2,1,0:T(8,128)S(1)}, u32[]{:S(2)}) copy-start(f32[5,2,64,4096]{3,2,1,0:T(8,128)S(1)} %maximum_select_fusion.9) | copy-start | bytes 31457284
  239.3 7.2 %copy-start = (f32[5,2,64,4096]{3,2,1,0:T(8,128)}, f32[5,2,64,4096]{3,2,1,0:T(8,128)S(1)}, u32[]{:S(2)}) copy-start(f32[5,2,64,4096]{3,2,1,0:T(8,128)S(1)} %maximum_select_fusion.10) | copy-start | bytes 31457284
  528.7 22.5 %collective-permute-start = (f32[5,1,64,512]{3,2,1,0:T(8,128)}, f32[5,1,64,512]{3,2,1,0:T(8,128)S(1)}, u32[]{:S(2)}, u32[]{:S(2)}) collective-permute-start(f32[5,1,64,512]{3,2,1,0:T(8,128)} %get-tuple-element.13), channel_id=1, source_target_pairs={{8,0},{16,8},{24,16},{9,1},{17,9},{25,17},{10,2},{18,10},{26,18},{... | collective-permute-start | bytes 1966088 | tf_op jit(solution)/shard_map/ppermute | solution.py:19
  530.0 21.2 %copy-start.4 = (f32[64]{0:T(128)S(1)}, f32[64]{0:T(128)}, u32[]{:S(2)}) copy-start(f32[64]{0:T(128)} %param.13) | copy-start | bytes 772
  530.0 21.2 %copy-start.5 = (f32[16]{0:T(128)S(1)}, f32[16]{0:T(128)}, u32[]{:S(2)}) copy-start(f32[16]{0:T(128)} %param.12) | copy-start | bytes 196
  530.0 21.2 %copy-start.6 = (f32[16]{0:T(128)S(1)}, f32[16]{0:T(128)}, u32[]{:S(2)}) copy-start(f32[16]{0:T(128)} %param.11) | copy-start | bytes 196
  530.0 21.2 %copy-start.7 = (f32[16]{0:T(128)S(1)}, f32[16]{0:T(128)}, u32[]{:S(2)}) copy-start(f32[16]{0:T(128)} %param.10) | copy-start | bytes 196
  530.0 21.2 %collective-permute-start.1 = (f32[5,1,64,512]{3,2,1,0:T(8,128)}, f32[5,1,64,512]{3,2,1,0:T(8,128)}, u32[]{:S(2)}, u32[]{:S(2)}) collective-permute-start(f32[5,1,64,512]{3,2,1,0:T(8,128)} %get-tuple-element.14), channel_id=1, source_target_pairs={{0,8},{8,16},{16,24},{1,9},{9,17},{17,25},{2,10},{10,18},{18,26},{... | collective-permute-start | bytes 1966088 | tf_op jit(solution)/shard_map/ppermute | solution.py:17
  543.6 1.7 collective-permute-start.2
  544.5 4.4 collective-permute-start.3
  585.6 8.2 %copy-start.3 = (f32[5,16,64,512]{3,2,1,0:T(8,128)}, f32[5,16,64,512]{3,2,1,0:T(8,128)S(1)}, u32[]{:S(2)}) copy-start(f32[5,16,64,512]{3,2,1,0:T(8,128)S(1)} %fusion.3) | copy-start | bytes 31457284
  586.9 19.7 %collective-permute-start.4 = (f32[5,1,64,512]{3,2,1,0:T(8,128)}, f32[5,1,64,512]{3,2,1,0:T(8,128)S(1)}, u32[]{:S(2)}, u32[]{:S(2)}) collective-permute-start(f32[5,1,64,512]{3,2,1,0:T(8,128)} %get-tuple-element.9), channel_id=1, source_target_pairs={{8,0},{16,8},{24,16},{9,1},{17,9},{25,17},{10,2},{18,10},{26,18},{... | collective-permute-start | bytes 1966088 | tf_op jit(solution)/shard_map/ppermute | solution.py:19
  588.1 18.4 %collective-permute-start.5 = (f32[5,1,64,512]{3,2,1,0:T(8,128)}, f32[5,1,64,512]{3,2,1,0:T(8,128)}, u32[]{:S(2)}, u32[]{:S(2)}) collective-permute-start(f32[5,1,64,512]{3,2,1,0:T(8,128)} %get-tuple-element.10), channel_id=1, source_target_pairs={{0,8},{8,16},{16,24},{1,9},{9,17},{17,25},{2,10},{10,18},{18,26},{... | collective-permute-start | bytes 1966088 | tf_op jit(solution)/shard_map/ppermute | solution.py:17
  598.9 1.7 collective-permute-start.6
  599.8 4.4 collective-permute-start.7
where the time goes:
time: 655 us; the launch traced here: 643 us
  local copies, waits for them, and re-layouts  205 us (31%)
  other arithmetic  171 us (26%)
  waiting for transfers between devices  123 us (19%)
  blocking collectives  123 us (19%)
  starting transfers between devices  20.5 us (3%)
    all_to_all x1, blocking collectives, local(): lax.all_to_all(shifted_loops, 'phi', split_axis=3, concat_axis=1, tiled=T...  123 us
    all_to_all x1, waiting for transfers between devices, local(): lax.all_to_all(fields, 'phi', split_axis=1, concat_axis=3, tiled=True)  117 us
    unnamed x23, local copies, waits for them, and re-layouts  78.3 us
    add x2, other arithmetic, combine(): return result + c_height * (above - 2.0 * state + below)  70.6 us
    select_n x12, other arithmetic, barrel_shift(): values = jnp.where(taken[None, :, None, None], rolled, values)  63.4 us
    all_to_all x1, other arithmetic, local(): lax.all_to_all(shifted_loops, 'phi', split_axis=3, concat_axis=1, tiled=T...  31.3 us
    all_to_all x2, local copies, waits for them, and re-layouts, local(): lax.all_to_all(fields, 'phi', split_axis=1, concat_axis=3, tiled=True)  26.4 us
    slice x18, local copies, waits for them, and re-layouts, barrel_shift(): rolled = jnp.roll(values, step_size, axis=3)  25.6 us
  transfers between devices with their start and end apart: 9, of which 5 were waited for; matrix products, arithmetic and copies ran while one was open for 3% of the time, Pallas kernels for 0%

commit v1 on v0

v1 whole, which is shorter than its diff:
```python
import functools

import jax
import jax.numpy as jnp
from jax import lax
from jax.experimental import pallas as pl
from jax.experimental.pallas import tpu as pltpu
from jax.sharding import PartitionSpec as P

LANES = 128
HALO = 2
MESH = pl.DeviceIdType.MESH


def kernel(
    n,
    rows,
    offs_ref,
    coef_ref,
    height_ref,
    fields_ref,
    out_ref,
    *scratch,
):
    fields, radii, nz, width = fields_ref.shape
    per = radii // n
    tiles = width // LANES
    loop_tiles = tiles * n
    (
        loops,
        stage,
        pack,
        edge_stage,
        state,
        edges,
        extra,
        mid,
        outb,
        coefs,
        in_send,
        in_recv,
        back_send,
        back_recv,
        edge_send,
        edge_recv,
        halo_send,
        halo_recv,
        coef_sem,
        own_sem,
        out_sem,
    ) = scratch
    me = lax.axis_index("phi")
    row = lax.axis_index("row")
    has_low = row > 0
    has_high = row < rows - 1
    lane = lax.broadcasted_iota(jnp.int32, (nz, LANES), 1)
    zrow = lax.broadcasted_iota(jnp.int32, (nz, LANES), 0)

    barrier = pltpu.get_barrier_semaphore()
    for d in range(1, n):
        pl.semaphore_signal(
            barrier, inc=1, device_id={"phi": lax.rem(me + d, n)}, device_id_type=MESH
        )

    @pl.when(has_low)
    def _():
        pl.semaphore_signal(barrier, inc=1, device_id={"row": row - 1}, device_id_type=MESH)

    @pl.when(has_high)
    def _():
        pl.semaphore_signal(barrier, inc=1, device_id={"row": row + 1}, device_id_type=MESH)

    inner = jnp.logical_and(has_low, has_high)

    @pl.when(inner)
    def _():
        pl.semaphore_wait(barrier, n + 1)

    @pl.when(jnp.logical_not(inner))
    def _():
        pl.semaphore_wait(barrier, n)

    def in_own(f):
        return pltpu.make_async_copy(
            fields_ref.at[f, pl.ds(me * per, per)], loops.at[f, me], own_sem.at[f]
        )

    def in_copy(f, d):
        to = lax.rem(me + d, n)
        return pltpu.make_async_remote_copy(
            src_ref=fields_ref.at[f, pl.ds(to * per, per)],
            dst_ref=loops.at[f, me],
            send_sem=in_send.at[f, d],
            recv_sem=in_recv.at[f, d],
            device_id={"phi": to},
            device_id_type=MESH,
        )

    def back_copies(f, d):
        to = lax.rem(me + d, n)
        main = pltpu.make_async_remote_copy(
            src_ref=stage.at[f, to],
            dst_ref=state.at[f, pl.ds(HALO + me * per, per)],
            send_sem=back_send.at[f, d],
            recv_sem=back_recv.at[f, d],
            device_id={"phi": to},
            device_id_type=MESH,
        )
        edge = pltpu.make_async_remote_copy(
            src_ref=edge_stage.at[f, to],
            dst_ref=edges.at[f, me + 1],
            send_sem=edge_send.at[f, d],
            recv_sem=edge_recv.at[f, d],
            device_id={"phi": to},
            device_id_type=MESH,
        )
        return main, edge

    def back_own(f):
        return (
            pltpu.make_async_copy(
                stage.at[f, me], state.at[f, pl.ds(HALO + me * per, per)], back_send.at[f, 0]
            ),
            pltpu.make_async_copy(edge_stage.at[f, me], edges.at[f, me + 1], edge_send.at[f, 0]),
        )

    def halo_copies(f, low):
        side = 0 if low else 1
        source = HALO if low else radii
        target = radii + HALO if low else 0
        to = row - 1 if low else row + 1
        return (
            pltpu.make_async_remote_copy(
                src_ref=state.at[f, pl.ds(source, HALO)],
                dst_ref=state.at[f, pl.ds(target, HALO)],
                send_sem=halo_send.at[f, side, 0],
                recv_sem=halo_recv.at[f, side, 0],
                device_id={"row": to},
                device_id_type=MESH,
            ),
            pltpu.make_async_remote_copy(
                src_ref=edges.at[f, 1 if low else n],
                dst_ref=edges.at[f, n + 1 if low else 0],
                send_sem=halo_send.at[f, side, 1],
                recv_sem=halo_recv.at[f, side, 1],
                device_id={"row": to},
                device_id_type=MESH,
            ),
        )

    def coef_copy(low):
        side = 0 if low else 1
        return pltpu.make_async_remote_copy(
            src_ref=coef_ref.at[pl.ds(0 if low else radii - HALO, HALO)],
            dst_ref=coefs.at[pl.ds(radii + HALO if low else 0, HALO)],
            send_sem=coef_sem.at[side],
            recv_sem=coef_sem.at[2 + side],
            device_id={"row": row - 1 if low else row + 1},
            device_id_type=MESH,
        )

    for f in range(fields):
        for d in range(1, n):
            in_copy(f, d).start()
        in_own(f).start()

    @pl.when(has_low)
    def _():
        coef_copy(True).start()

    @pl.when(has_high)
    def _():
        coef_copy(False).start()

    coefs[pl.ds(HALO, radii)] = coef_ref[...]

    @pl.when(jnp.logical_not(has_low))
    def _():
        state[:, 0:HALO] = jnp.zeros((fields, HALO, nz, width), jnp.float32)
        edges[:, 0] = jnp.zeros(edges.shape[:1] + edges.shape[2:], jnp.float32)
        coefs[0:HALO] = jnp.zeros((HALO,) + coefs.shape[1:], jnp.float32)

    @pl.when(jnp.logical_not(has_high))
    def _():
        state[:, radii + HALO :] = jnp.zeros((fields, HALO, nz, width), jnp.float32)
        edges[:, n + 1] = jnp.zeros(edges.shape[:1] + edges.shape[2:], jnp.float32)
        coefs[radii + HALO :] = jnp.zeros((HALO,) + coefs.shape[1:], jnp.float32)

    lane8 = lax.broadcasted_iota(jnp.int32, (8, LANES), 1)

    def shift_field(f, carry):
        in_own(f).wait()
        for d in range(1, n):
            in_copy(f, d).wait_recv()

        def shift_loop(ri, carry):
            offset = jnp.broadcast_to(offs_ref[me * per + ri, 0:1, :], (8, LANES))
            weight = jnp.broadcast_to(coef_ref[me * per + ri, 4:5, :], (8, LANES))
            keep = 1.0 - weight
            fine = offset & (LANES - 1)

            def shift_rows(group, carry):
                z0 = pl.multiple_of(group * 8, 8)
                cells = [
                    loops[f, t // tiles, ri, pl.ds(z0, 8), (t % tiles) * LANES : (t % tiles + 1) * LANES]
                    for t in range(loop_tiles)
                ]
                step = 1
                while step < LANES:
                    taken = (offset & step) != 0
                    cells = [jnp.where(taken, pltpu.roll(c, step, 1), c) for c in cells]
                    step *= 2
                inside = lane8 < fine
                cells = [
                    jnp.where(inside, cells[t - 1], cells[t]) for t in range(loop_tiles)
                ]
                step = 1
                while step < loop_tiles:
                    taken = (offset & (step * LANES)) != 0
                    cells = [
                        jnp.where(taken, cells[t - step], cells[t]) for t in range(loop_tiles)
                    ]
                    step *= 2
                turned = [pltpu.roll(c, 1, 1) for c in cells]
                moved = [
                    keep * cells[t] + weight * jnp.where(lane8 == 0, turned[t - 1], turned[t])
                    for t in range(loop_tiles)
                ]
                for t in range(loop_tiles):
                    at = (t % tiles) * LANES
                    stage[f, t // tiles, ri, pl.ds(z0, 8), at : at + LANES] = moved[t]
                for q in range(n):
                    right = moved[(tiles * q + tiles) % loop_tiles]
                    both = jnp.where(lane8 < LANES // 2, right, moved[tiles * q - 1])
                    pack[ri, q, pl.ds(z0, 8), :] = both
                return carry

            return lax.fori_loop(0, nz // 8, shift_rows, carry)

        lax.fori_loop(0, per, shift_loop, 0)

        def pack_edges(q, carry):
            tile = pltpu.roll(pack[0, q], 2, 1)
            for ri in range(1, per):
                tile = jnp.where(lane < 4 * ri, tile, pltpu.roll(pack[ri, q], 2 + 4 * ri, 1))
            square = jnp.concatenate([tile] * (LANES // nz), axis=0).T
            edge_stage[f, q] = square[0 : 4 * per]
            return carry

        lax.fori_loop(0, n, pack_edges, 0)
        for copy in back_own(f):
            copy.start()
        for d in range(1, n):
            for copy in back_copies(f, d):
                copy.start()
        return carry

    lax.fori_loop(0, fields, shift_field, 0)

    @pl.when(has_low)
    def _():
        coef_copy(False).wait_recv()

    @pl.when(has_high)
    def _():
        coef_copy(True).wait_recv()

    def blend(cur, prev_tile, next_tile, up, low, where_r, height, height2):
        k_up = coefs[where_r, 0:1, :]
        k_low = coefs[where_r, 1:2, :]
        k_loop = coefs[where_r, 2:3, :]
        k_mid = coefs[where_r, 3:4, :]
        west = jnp.where(lane == 0, pltpu.roll(prev_tile, 1, 1), pltpu.roll(cur, 1, 1))
        east = jnp.where(
            lane == LANES - 1,
            pltpu.roll(next_tile, LANES - 1, 1),
            pltpu.roll(cur, LANES - 1, 1),
        )
        below = jnp.where(zrow == 0, 0.0, pltpu.roll(cur, 1, 0))
        above = jnp.where(zrow == nz - 1, 0.0, pltpu.roll(cur, nz - 1, 0))
        total = (k_mid - height2) * cur + k_up * up + k_low * low
        return total + k_loop * (east + west) + height * (above + below)

    def out_copy(f):
        return pltpu.make_async_copy(outb.at[f % 2], out_ref.at[f], out_sem.at[f % 2])

    for f in range(fields):
        for copy in back_own(f):
            copy.wait()
        for d in range(1, n):
            for copy in back_copies(f, d):
                copy.wait_recv()

        @pl.when(has_low)
        def _(f=f):
            for copy in halo_copies(f, True):
                copy.start()

        @pl.when(has_high)
        def _(f=f):
            for copy in halo_copies(f, False):
                copy.start()

        @pl.when(has_low)
        def _(f=f):
            for copy in halo_copies(f, False):
                copy.wait_recv()

        @pl.when(has_high)
        def _(f=f):
            for copy in halo_copies(f, True):
                copy.wait_recv()

        lines = edges[f].reshape((n + 2) * 4 * per, LANES)
        square = jnp.concatenate([lines, lines[0 : LANES - lines.shape[0]]], axis=0).T[0:nz]

        def spread(i, carry):
            extra[i] = pltpu.roll(square, LANES - 2 - 4 * i, 1)
            return carry

        lax.fori_loop(0, radii + 2 * HALO, spread, 0)

        def first(i, carry, f=f):
            height = height_ref[...]
            height2 = height + height

            def tile(r, t):
                if t == tiles:
                    return extra[r]
                return state[f, r, :, pl.ds(t * LANES, LANES)]

            for t in range(tiles + 1):
                mid[i - 1, :, pl.ds(t * LANES, LANES)] = blend(
                    tile(i, t),
                    tile(i, (t + tiles) % (tiles + 1)),
                    tile(i, (t + 1) % (tiles + 1)),
                    tile(i + 1, t),
                    tile(i - 1, t),
                    i,
                    height,
                    height2,
                )
            return carry

        lax.fori_loop(1, radii + 2 * HALO - 1, first, 0)

        @pl.when(jnp.logical_not(has_low))
        def _():
            mid[0] = jnp.zeros(mid.shape[1:], jnp.float32)

        @pl.when(jnp.logical_not(has_high))
        def _():
            mid[radii + 1] = jnp.zeros(mid.shape[1:], jnp.float32)

        if f >= 2:
            out_copy(f - 2).wait()

        def second(i, carry, f=f):
            height = height_ref[...]
            height2 = height + height

            def tile(r, t):
                return mid[r, :, pl.ds(t * LANES, LANES)]

            for t in range(tiles):
                outb[f % 2, i - 1, :, pl.ds(t * LANES, LANES)] = blend(
                    tile(i, t),
                    tile(i, (t + tiles) % (tiles + 1)),
                    tile(i, (t + 1) % (tiles + 1)),
                    tile(i + 1, t),
                    tile(i - 1, t),
                    i + 1,
                    height,
                    height2,
                )
            return carry

        lax.fori_loop(1, radii + 1, second, 0)
        out_copy(f).start()

    for f in range(max(fields - 2, 0), fields):
        out_copy(f).wait()
    for f in range(fields):
        for d in range(1, n):
            in_copy(f, d).wait_send()
            for copy in back_copies(f, d):
                copy.wait_send()

        @pl.when(has_low)
        def _(f=f):
            for copy in halo_copies(f, True):
                copy.wait_send()

        @pl.when(has_high)
        def _(f=f):
            for copy in halo_copies(f, False):
                copy.wait_send()

    @pl.when(has_low)
    def _():
        coef_copy(True).wait_send()

    @pl.when(has_high)
    def _():
        coef_copy(False).wait_send()


def local(n, rows, fields, offsets, fraction, radial_diff, radial_drift, loop_diff, height_diff):
    count, radii, nz, width = fields.shape
    per = radii // n
    full = radii + 2 * HALO
    wide = width + LANES
    table = jnp.stack(
        [
            radial_diff + radial_drift,
            radial_diff - radial_drift,
            loop_diff,
            1.0 - 2.0 * (radial_diff + loop_diff),
            fraction,
        ],
        axis=1,
    )
    table = jnp.pad(table, ((0, 0), (0, 3)))
    table = jnp.broadcast_to(table[:, :, None], (radii, 8, LANES))
    shifts = jnp.broadcast_to(offsets[:, None, None], (radii, 8, LANES))
    heights = jnp.broadcast_to(height_diff[:, None], (nz, LANES))
    f32 = jnp.float32
    dma = pltpu.SemaphoreType.DMA
    scratch = [
        pltpu.VMEM((count, n, per, nz, width), f32),
        pltpu.VMEM((count, n, per, nz, width), f32),
        pltpu.VMEM((per, n, nz, LANES), f32),
        pltpu.VMEM((count, n, 4 * per, LANES), f32),
        pltpu.VMEM((count, full, nz, width), f32),
        pltpu.VMEM((count, n + 2, 4 * per, LANES), f32),
        pltpu.VMEM((full, nz, LANES), f32),
        pltpu.VMEM((full - 2, nz, wide), f32),
        pltpu.VMEM((2, radii, nz, width), f32),
        pltpu.VMEM((full, 8, LANES), f32),
        dma((count, n)),
        dma((count, n)),
        dma((count, n)),
        dma((count, n)),
        dma((count, n)),
        dma((count, n)),
        dma((count, 2, 2)),
        dma((count, 2, 2)),
        dma((4,)),
        dma((count,)),
        dma((2,)),
    ]
    vmem = pl.BlockSpec(memory_space=pltpu.VMEM)
    hbm = pl.BlockSpec(memory_space=pl.ANY)
    return pl.pallas_call(
        functools.partial(kernel, n, rows),
        out_shape=jax.ShapeDtypeStruct(fields.shape, f32),
        in_specs=[vmem, vmem, vmem, hbm],
        out_specs=hbm,
        scratch_shapes=scratch,
        compiler_params=pltpu.CompilerParams(
            collective_id=0, has_side_effects=True, vmem_limit_bytes=60 * 1024 * 1024
        ),
    )(shifts, table, heights, fields)


def solution(mesh):
    placed = (P(None, "row", None, "phi"), P("row"), P("row"), P("row"), P("row"), P("row"), P())
    body = functools.partial(local, mesh.shape["phi"], mesh.shape["row"])
    return jax.shard_map(
        body, mesh=mesh, in_specs=placed, out_specs=P(None, "row", None, "phi"), check_vma=False
    )
```

time: 655 us -> 267 us (0.41); the launches traced: 643 us -> 263 us
  Pallas kernels: 0 us -> 248 us
  local copies, waits for them, and re-layouts: 205 us -> 14.6 us
  other arithmetic: 171 us -> 0.69 us
  blocking collectives: 123 us -> 0 us
  waiting for transfers between devices: 123 us -> 0 us
  starting transfers between devices: 20.5 us -> 0 us
    pallas_call x0 -> x1, Pallas kernels: none -> 248 us  [local(): pl.pallas_call(functools.partial(kernel, n, rows), out_shape=jax.ShapeDty...]
    all_to_all x1 -> x0, blocking collectives: 123 us -> none  [local(): lax.all_to_all(shifted_loops, 'phi', split_axis=3, concat_axis=1, tiled=T...]
    all_to_all x1 -> x0, waiting for transfers between devices: 117 us -> none  [local(): lax.all_to_all(fields, 'phi', split_axis=1, concat_axis=3, tiled=True)]
    add x3 -> x0, other arithmetic: 76.1 us -> none  [the longest x2 70.6 us: combine(): return result + c_height * (above - 2.0 * state + below)]
    unnamed x23 -> x2, local copies, waits for them, and re-layouts: 78.3 us -> 10.5 us
    select_n x12 -> x0, other arithmetic: 63.4 us -> none  [barrel_shift(): values = jnp.where(taken[None, :, None, None], rolled, values)]
    all_to_all x4 -> x0, local copies, waits for them, and re-layouts: 51.9 us -> none  [the longest x2 26.4 us: local(): lax.all_to_all(fields, 'phi', split_axis=1, concat_axis=3, tiled=True)]
    slice x27 -> x0, local copies, waits for them, and re-layouts: 44 us -> none  [the longest x18 25.6 us: barrel_shift(): rolled = jnp.roll(values, step_size, axis=3)]
  transfers between devices with their start and end apart: 9 -> 0, of which waited for: 5 -> 0; matrix products, arithmetic and copies ran while one was open for 3% -> 0% of each run, Pallas kernels for 0% -> 0%
where the time goes in v1:
time: 267 us; the launch traced here: 263 us
  Pallas kernels  248 us (93%)
  local copies, waits for them, and re-layouts  14.6 us (5%)
    pallas_call x1, Pallas kernels, local(): pl.pallas_call(functools.partial(kernel, n, rows), out_shape=jax.ShapeDty...  248 us
    unnamed x2, local copies, waits for them, and re-layouts  10.5 us

profile of v1, /device:TPU:0, one launch (start us, length us, event | category | flops | bytes accessed | tf_op | source)
XLA Modules:
  0.0 263.2 jit_solution(3996315672766753518)
XLA Ops:
  0.0 0.7 subtract_bitcast_fusion.1
  0.7 0.7 stack.23
  1.4 0.1 copy.9
  1.5 1.3 broadcast_in_dim.8.height_ref
  2.8 0.7 broadcast_in_dim.7.coef_ref
  3.5 1.4 broadcast_in_dim.6.offs_ref
  4.9 247.9 %shard_map.73 = f32[5,16,64,512]{3,2,1,0:T(8,128)} custom-call(s32[16,8,128]{2,1,0:T(8,128)} %broadcast_in_dim.6.offs_ref, f32[16,8,128]{2,1,0:T(8,128)} %broadcast_in_dim.7.coef_ref, f32[64,128]{1,0:T(8,128)} %broadcast_in_dim.8.height_ref, f32[5,16,64,512]{3,2,1,0:T(8,128)} %fields_ref.1), custom_call_target="tpu_custom_call" | custom-call | tf_op jit(solution)/shard_map/pallas_call | solution.py:454
  252.8 10.4 %copy.11 = f32[5,16,64,512]{3,2,1,0:T(8,128)} copy(f32[5,16,64,512]{3,2,1,0:T(8,128)} %shard_map.73) | data formatting | bytes 20971520
  (1 shorter events, 0.0 us)

commit v2 on v1

--- a/solution.py
+++ b/solution.py
@@ -15,9 +15,12 @@
 def kernel(
     n,
     rows,
-    offs_ref,
-    coef_ref,
-    height_ref,
+    offs_in,
+    frac_in,
+    diff_in,
+    drift_in,
+    loop_in,
+    rise_in,
     fields_ref,
     out_ref,
     *scratch,
@@ -35,8 +38,15 @@
         edges,
         extra,
         mid,
-        outb,
         coefs,
+        height_ref,
+        offs_ref,
+        frac_ref,
+        diff_ref,
+        drift_ref,
+        loop_ref,
+        rise_ref,
+        small_sem,
         in_send,
         in_recv,
         back_send,
@@ -47,8 +57,22 @@
         halo_recv,
         coef_sem,
         own_sem,
-        out_sem,
     ) = scratch
+    smalls = [
+        pltpu.make_async_copy(source, target, small_sem.at[i])
+        for i, (source, target) in enumerate(
+            (
+                (offs_in, offs_ref),
+                (frac_in, frac_ref),
+                (diff_in, diff_ref),
+                (drift_in, drift_ref),
+                (loop_in, loop_ref),
+                (rise_in, rise_ref),
+            )
+        )
+    ]
+    for copy in smalls:
+        copy.start()
     me = lax.axis_index("phi")
     row = lax.axis_index("row")
     has_low = row > 0
@@ -151,7 +175,7 @@
     def coef_copy(low):
         side = 0 if low else 1
         return pltpu.make_async_remote_copy(
-            src_ref=coef_ref.at[pl.ds(0 if low else radii - HALO, HALO)],
+            src_ref=coefs.at[pl.ds(HALO if low else radii, HALO)],
             dst_ref=coefs.at[pl.ds(radii + HALO if low else 0, HALO)],
             send_sem=coef_sem.at[side],
             recv_sem=coef_sem.at[2 + side],
@@ -164,6 +188,29 @@
             in_copy(f, d).start()
         in_own(f).start()
 
+    for copy in smalls:
+        copy.wait()
+
+    def fill_coefs(i, carry):
+        diff = jnp.full((1, LANES), diff_ref[i], jnp.float32)
+        drift = jnp.full((1, LANES), drift_ref[i], jnp.float32)
+        loop = jnp.full((1, LANES), loop_ref[i], jnp.float32)
+        coefs[HALO + i, 0:1, :] = diff + drift
+        coefs[HALO + i, 1:2, :] = diff - drift
+        coefs[HALO + i, 2:3, :] = loop
+        coefs[HALO + i, 3:4, :] = 1.0 - 2.0 * (diff + loop)
+        coefs[HALO + i, 4:5, :] = jnp.full((1, LANES), frac_ref[i], jnp.float32)
+        coefs[HALO + i, 5:8, :] = jnp.zeros((3, LANES), jnp.float32)
+        return carry
+
+    lax.fori_loop(0, radii, fill_coefs, 0)
+
+    def fill_height(z, carry):
+        height_ref[pl.ds(z, 1), :] = jnp.full((1, LANES), rise_ref[z], jnp.float32)
+        return carry
+
+    lax.fori_loop(0, nz, fill_height, 0)
+
     @pl.when(has_low)
     def _():
         coef_copy(True).start()
@@ -172,7 +219,6 @@
     def _():
         coef_copy(False).start()
 
-    coefs[pl.ds(HALO, radii)] = coef_ref[...]
 
     @pl.when(jnp.logical_not(has_low))
     def _():
@@ -194,8 +240,8 @@
             in_copy(f, d).wait_recv()
 
         def shift_loop(ri, carry):
-            offset = jnp.broadcast_to(offs_ref[me * per + ri, 0:1, :], (8, LANES))
-            weight = jnp.broadcast_to(coef_ref[me * per + ri, 4:5, :], (8, LANES))
+            offset = jnp.full((8, LANES), offs_ref[me * per + ri], jnp.int32)
+            weight = jnp.broadcast_to(coefs[HALO + me * per + ri, 4:5, :], (8, LANES))
             keep = 1.0 - weight
             fine = offset & (LANES - 1)
 
@@ -281,9 +327,6 @@
         total = (k_mid - height2) * cur + k_up * up + k_low * low
         return total + k_loop * (east + west) + height * (above + below)
 
-    def out_copy(f):
-        return pltpu.make_async_copy(outb.at[f % 2], out_ref.at[f], out_sem.at[f % 2])
-
     for f in range(fields):
         for copy in back_own(f):
             copy.wait()
@@ -352,9 +395,6 @@
         def _():
             mid[radii + 1] = jnp.zeros(mid.shape[1:], jnp.float32)
 
-        if f >= 2:
-            out_copy(f - 2).wait()
-
         def second(i, carry, f=f):
             height = height_ref[...]
             height2 = height + height
@@ -363,7 +403,7 @@
                 return mid[r, :, pl.ds(t * LANES, LANES)]
 
             for t in range(tiles):
-                outb[f % 2, i - 1, :, pl.ds(t * LANES, LANES)] = blend(
+                out_ref[f, i - 1, :, pl.ds(t * LANES, LANES)] = blend(
                     tile(i, t),
                     tile(i, (t + tiles) % (tiles + 1)),
                     tile(i, (t + 1) % (tiles + 1)),
@@ -376,10 +416,7 @@
             return carry
 
         lax.fori_loop(1, radii + 1, second, 0)
-        out_copy(f).start()
-
-    for f in range(max(fields - 2, 0), fields):
-        out_copy(f).wait()
+
     for f in range(fields):
         for d in range(1, n):
             in_copy(f, d).wait_send()
@@ -410,20 +447,6 @@
     per = radii // n
     full = radii + 2 * HALO
     wide = width + LANES
-    table = jnp.stack(
-        [
-            radial_diff + radial_drift,
-            radial_diff - radial_drift,
-            loop_diff,
-            1.0 - 2.0 * (radial_diff + loop_diff),
-            fraction,
-        ],
-        axis=1,
-    )
-    table = jnp.pad(table, ((0, 0), (0, 3)))
-    table = jnp.broadcast_to(table[:, :, None], (radii, 8, LANES))
-    shifts = jnp.broadcast_to(offsets[:, None, None], (radii, 8, LANES))
-    heights = jnp.broadcast_to(height_diff[:, None], (nz, LANES))
     f32 = jnp.float32
     dma = pltpu.SemaphoreType.DMA
     scratch = [
@@ -435,8 +458,15 @@
         pltpu.VMEM((count, n + 2, 4 * per, LANES), f32),
         pltpu.VMEM((full, nz, LANES), f32),
         pltpu.VMEM((full - 2, nz, wide), f32),
-        pltpu.VMEM((2, radii, nz, width), f32),
         pltpu.VMEM((full, 8, LANES), f32),
+        pltpu.VMEM((nz, LANES), f32),
+        pltpu.SMEM((radii,), jnp.int32),
+        pltpu.SMEM((radii,), f32),
+        pltpu.SMEM((radii,), f32),
+        pltpu.SMEM((radii,), f32),
+        pltpu.SMEM((radii,), f32),
+        pltpu.SMEM((nz,), f32),
+        dma((6,)),
         dma((count, n)),
         dma((count, n)),
         dma((count, n)),
@@ -447,20 +477,18 @@
         dma((count, 2, 2)),
         dma((4,)),
         dma((count,)),
-        dma((2,)),
     ]
-    vmem = pl.BlockSpec(memory_space=pltpu.VMEM)
-    hbm = pl.BlockSpec(memory_space=pl.ANY)
+    hbm = pl.BlockSpec(memory_space=pltpu.HBM)
     return pl.pallas_call(
         functools.partial(kernel, n, rows),
-        out_shape=jax.ShapeDtypeStruct(fields.shape, f32),
-        in_specs=[vmem, vmem, vmem, hbm],
-        out_specs=hbm,
+        out_shape=pltpu.VMEM(fields.shape, f32),
+        in_specs=[hbm] * 7,
+        out_specs=pl.BlockSpec(memory_space=pltpu.VMEM),
         scratch_shapes=scratch,
         compiler_params=pltpu.CompilerParams(
-            collective_id=0, has_side_effects=True, vmem_limit_bytes=60 * 1024 * 1024
+            collective_id=0, has_side_effects=True, vmem_limit_bytes=42 * 1024 * 1024
         ),
-    )(shifts, table, heights, fields)
+    )(offsets, fraction, radial_diff, radial_drift, loop_diff, height_diff, fields)
 
 
 def solution(mesh):

time: 267 us -> 258 us (0.966)
  local copies, waits for them, and re-layouts: 14.6 us -> 8.02 us
    broadcast_in_dim x3 -> x0, local copies, waits for them, and re-layouts: 3.41 us -> none  [the longest x1 1.37 us: local(): shifts = jnp.broadcast_to(offsets[:, None, None], (radii, 8, LANES))]
    unnamed x2 -> x13, local copies, waits for them, and re-layouts: 10.5 us -> 8.02 us
where the time goes in v2:
time: 258 us; the launch traced here: 254 us
  Pallas kernels  246 us (95%)
  local copies, waits for them, and re-layouts  8.02 us (3%)
    pallas_call x1, Pallas kernels, local(): pl.pallas_call(functools.partial(kernel, n, rows), out_shape=pltpu.VMEM(f...  246 us
    unnamed x13, local copies, waits for them, and re-layouts  8.02 us

profile of v2, /device:TPU:0, one launch (start us, length us, event | category | flops | bytes accessed | tf_op | source)
XLA Modules:
  0.0 253.8 jit_solution(18215410563224247317)
XLA Ops:
  0.0 0.0 copy-start
  0.0 0.7 copy-done
  0.7 0.0 copy-start.1
  0.7 0.7 copy-done.1
  1.3 0.0 copy-start.2
  1.3 0.7 copy-done.2
  2.0 0.0 copy-start.3
  2.0 0.7 copy-done.3
  2.6 0.0 copy-start.4
  2.6 0.7 copy-done.4
  3.3 0.0 copy-start.5
  3.3 0.7 copy-done.5
  3.9 245.7 %shard_map.73 = f32[5,16,64,512]{3,2,1,0:T(8,128)S(1)} custom-call(s32[16]{0:T(128)S(1)} %copy-done, f32[16]{0:T(128)S(1)} %copy-done.1, f32[16]{0:T(128)S(1)} %copy-done.2, f32[16]{0:T(128)S(1)} %copy-done.3, f32[16]{0:T(128)S(1)} %copy-done.4, f32[64]{0:T(128)S(1)} %copy-done.5, f32[5,16,64,512]{3,2,1,0:T(8,128)} %fields_ref.1), custom_call_target="tpu_custom_call" | custom-call | tf_op jit(solution)/shard_map/pallas_call | solution.py:482
  249.7 4.1 %copy.9 = f32[5,16,64,512]{3,2,1,0:T(8,128)} copy(f32[5,16,64,512]{3,2,1,0:T(8,128)S(1)} %shard_map.73) | data formatting | bytes 20971520
Async XLA Ops:
  0.0 0.7 copy-start
  0.7 0.7 copy-start.1
  1.3 0.7 copy-start.2
  2.0 0.7 copy-start.3
  2.6 0.7 copy-start.4
  3.3 0.7 copy-start.5

commit v3 on v2

--- a/solution.py
+++ b/solution.py
@@ -27,6 +27,7 @@
 ):
     fields, radii, nz, width = fields_ref.shape
     per = radii // n
+    half = n // 2
     tiles = width // LANES
     loop_tiles = tiles * n
     (
@@ -104,48 +105,57 @@
     def _():
         pl.semaphore_wait(barrier, n)
 
-    def in_own(f):
+    def radius(owner, ri):
+        if ri == 1:
+            return owner + half
+        return jnp.where(owner < half, owner, owner + radii - n)
+
+    def in_own(f, ri):
         return pltpu.make_async_copy(
-            fields_ref.at[f, pl.ds(me * per, per)], loops.at[f, me], own_sem.at[f]
-        )
-
-    def in_copy(f, d):
+            fields_ref.at[f, radius(me, ri)], loops.at[f, me, ri], own_sem.at[f, ri]
+        )
+
+    def in_copy(f, ri, d):
         to = lax.rem(me + d, n)
         return pltpu.make_async_remote_copy(
-            src_ref=fields_ref.at[f, pl.ds(to * per, per)],
-            dst_ref=loops.at[f, me],
-            send_sem=in_send.at[f, d],
-            recv_sem=in_recv.at[f, d],
+            src_ref=fields_ref.at[f, radius(to, ri)],
+            dst_ref=loops.at[f, me, ri],
+            send_sem=in_send.at[f, ri, d],
+            recv_sem=in_recv.at[f, ri, d],
             device_id={"phi": to},
             device_id_type=MESH,
         )
 
-    def back_copies(f, d):
+    def back_copy(f, ri, d):
         to = lax.rem(me + d, n)
-        main = pltpu.make_async_remote_copy(
-            src_ref=stage.at[f, to],
-            dst_ref=state.at[f, pl.ds(HALO + me * per, per)],
-            send_sem=back_send.at[f, d],
-            recv_sem=back_recv.at[f, d],
+        return pltpu.make_async_remote_copy(
+            src_ref=stage.at[f, to, ri],
+            dst_ref=state.at[f, HALO + radius(me, ri)],
+            send_sem=back_send.at[f, ri, d],
+            recv_sem=back_recv.at[f, ri, d],
             device_id={"phi": to},
             device_id_type=MESH,
         )
-        edge = pltpu.make_async_remote_copy(
+
+    def edge_copy(f, d):
+        to = lax.rem(me + d, n)
+        return pltpu.make_async_remote_copy(
             src_ref=edge_stage.at[f, to],
-            dst_ref=edges.at[f, me + 1],
+            dst_ref=edges.at[f, me + HALO],
             send_sem=edge_send.at[f, d],
             recv_sem=edge_recv.at[f, d],
             device_id={"phi": to},
             device_id_type=MESH,
         )
-        return main, edge
-
-    def back_own(f):
-        return (
-            pltpu.make_async_copy(
-                stage.at[f, me], state.at[f, pl.ds(HALO + me * per, per)], back_send.at[f, 0]
-            ),
-            pltpu.make_async_copy(edge_stage.at[f, me], edges.at[f, me + 1], edge_send.at[f, 0]),
+
+    def back_own(f, ri):
+        return pltpu.make_async_copy(
+            stage.at[f, me, ri], state.at[f, HALO + radius(me, ri)], back_send.at[f, ri, 0]
+        )
+
+    def edge_own(f):
+        return pltpu.make_async_copy(
+            edge_stage.at[f, me], edges.at[f, me + HALO], edge_send.at[f, 0]
         )
 
     def halo_copies(f, low):
@@ -163,8 +173,8 @@
                 device_id_type=MESH,
             ),
             pltpu.make_async_remote_copy(
-                src_ref=edges.at[f, 1 if low else n],
-                dst_ref=edges.at[f, n + 1 if low else 0],
+                src_ref=edges.at[f, pl.ds(HALO if low else n, HALO)],
+                dst_ref=edges.at[f, pl.ds(n + HALO if low else 0, HALO)],
                 send_sem=halo_send.at[f, side, 1],
                 recv_sem=halo_recv.at[f, side, 1],
                 device_id={"row": to},
@@ -184,9 +194,10 @@
         )
 
     for f in range(fields):
-        for d in range(1, n):
-            in_copy(f, d).start()
-        in_own(f).start()
+        for ri in range(per):
+            for d in range(1, n):
+                in_copy(f, ri, d).start()
+            in_own(f, ri).start()
 
     for copy in smalls:
         copy.wait()
@@ -223,25 +234,27 @@
     @pl.when(jnp.logical_not(has_low))
     def _():
         state[:, 0:HALO] = jnp.zeros((fields, HALO, nz, width), jnp.float32)
-        edges[:, 0] = jnp.zeros(edges.shape[:1] + edges.shape[2:], jnp.float32)
+        edges[:, 0:HALO] = jnp.zeros((fields, HALO) + edges.shape[2:], jnp.float32)
         coefs[0:HALO] = jnp.zeros((HALO,) + coefs.shape[1:], jnp.float32)
 
     @pl.when(jnp.logical_not(has_high))
     def _():
         state[:, radii + HALO :] = jnp.zeros((fields, HALO, nz, width), jnp.float32)
-        edges[:, n + 1] = jnp.zeros(edges.shape[:1] + edges.shape[2:], jnp.float32)
+        edges[:, n + HALO :] = jnp.zeros((fields, HALO) + edges.shape[2:], jnp.float32)
         coefs[radii + HALO :] = jnp.zeros((HALO,) + coefs.shape[1:], jnp.float32)
 
     lane8 = lax.broadcasted_iota(jnp.int32, (8, LANES), 1)
 
     def shift_field(f, carry):
-        in_own(f).wait()
-        for d in range(1, n):
-            in_copy(f, d).wait_recv()
+        for ri in range(per):
+            in_own(f, ri).wait()
+            for d in range(1, n):
+                in_copy(f, ri, d).wait_recv()
 
         def shift_loop(ri, carry):
-            offset = jnp.full((8, LANES), offs_ref[me * per + ri], jnp.int32)
-            weight = jnp.broadcast_to(coefs[HALO + me * per + ri, 4:5, :], (8, LANES))
+            mine = jnp.where(ri == 0, radius(me, 0), radius(me, 1))
+            offset = jnp.full((8, LANES), offs_ref[mine], jnp.int32)
+            weight = jnp.broadcast_to(coefs[HALO + mine, 4:5, :], (8, LANES))
             keep = 1.0 - weight
             fine = offset & (LANES - 1)
 
@@ -294,11 +307,13 @@
             return carry
 
         lax.fori_loop(0, n, pack_edges, 0)
-        for copy in back_own(f):
-            copy.start()
+        edge_own(f).start()
         for d in range(1, n):
-            for copy in back_copies(f, d):
-                copy.start()
+            edge_copy(f, d).start()
+        for ri in range(per):
+            back_own(f, ri).start()
+            for d in range(1, n):
+                back_copy(f, ri, d).start()
         return carry
 
     lax.fori_loop(0, fields, shift_field, 0)
@@ -328,11 +343,11 @@
         return total + k_loop * (east + west) + height * (above + below)
 
     for f in range(fields):
-        for copy in back_own(f):
-            copy.wait()
+        edge_own(f).wait()
+        back_own(f, 0).wait()
         for d in range(1, n):
-            for copy in back_copies(f, d):
-                copy.wait_recv()
+            edge_copy(f, d).wait_recv()
+            back_copy(f, 0, d).wait_recv()
 
         @pl.when(has_low)
         def _(f=f):
@@ -354,14 +369,17 @@
             for copy in halo_copies(f, True):
                 copy.wait_recv()
 
-        lines = edges[f].reshape((n + 2) * 4 * per, LANES)
+        lines = edges[f].reshape((n + 2 * HALO) * 4 * per, LANES)
         square = jnp.concatenate([lines, lines[0 : LANES - lines.shape[0]]], axis=0).T[0:nz]
-
-        def spread(i, carry):
-            extra[i] = pltpu.roll(square, LANES - 2 - 4 * i, 1)
-            return carry
-
-        lax.fori_loop(0, radii + 2 * HALO, spread, 0)
+        for i in range(radii + 2 * HALO):
+            r = i - HALO
+            if r < half:
+                at = 8 * i
+            elif r < half + n:
+                at = 8 * (HALO + r - half) + 4
+            else:
+                at = 8 * (HALO + r - radii + n)
+            extra[i] = pltpu.roll(square, (2 * LANES - 2 - at) % LANES, 1)
 
         def first(i, carry, f=f):
             height = height_ref[...]
@@ -385,7 +403,8 @@
                 )
             return carry
 
-        lax.fori_loop(1, radii + 2 * HALO - 1, first, 0)
+        lax.fori_loop(1, half + 1, first, 0)
+        lax.fori_loop(radii + 2 * HALO - 1 - half, radii + 2 * HALO - 1, first, 0)
 
         @pl.when(jnp.logical_not(has_low))
         def _():
@@ -415,13 +434,20 @@
                 )
             return carry
 
-        lax.fori_loop(1, radii + 1, second, 0)
+        lax.fori_loop(1, half - 1, second, 0)
+        lax.fori_loop(radii - half + 3, radii + 1, second, 0)
+        back_own(f, 1).wait()
+        for d in range(1, n):
+            back_copy(f, 1, d).wait_recv()
+        lax.fori_loop(half + 1, radii + 2 * HALO - 1 - half, first, 0)
+        lax.fori_loop(half - 1, radii - half + 3, second, 0)
 
     for f in range(fields):
         for d in range(1, n):
-            in_copy(f, d).wait_send()
-            for copy in back_copies(f, d):
-                copy.wait_send()
+            edge_copy(f, d).wait_send()
+            for ri in range(per):
+                in_copy(f, ri, d).wait_send()
+                back_copy(f, ri, d).wait_send()
 
         @pl.when(has_low)
         def _(f=f):
@@ -455,7 +481,7 @@
         pltpu.VMEM((per, n, nz, LANES), f32),
         pltpu.VMEM((count, n, 4 * per, LANES), f32),
         pltpu.VMEM((count, full, nz, width), f32),
-        pltpu.VMEM((count, n + 2, 4 * per, LANES), f32),
+        pltpu.VMEM((count, n + 2 * HALO, 4 * per, LANES), f32),
         pltpu.VMEM((full, nz, LANES), f32),
         pltpu.VMEM((full - 2, nz, wide), f32),
         pltpu.VMEM((full, 8, LANES), f32),
@@ -467,16 +493,16 @@
         pltpu.SMEM((radii,), f32),
         pltpu.SMEM((nz,), f32),
         dma((6,)),
-        dma((count, n)),
-        dma((count, n)),
-        dma((count, n)),
-        dma((count, n)),
+        dma((count, per, n)),
+        dma((count, per, n)),
+        dma((count, per, n)),
+        dma((count, per, n)),
         dma((count, n)),
         dma((count, n)),
         dma((count, 2, 2)),
         dma((count, 2, 2)),
         dma((4,)),
-        dma((count,)),
+        dma((count, per)),
     ]
     hbm = pl.BlockSpec(memory_space=pltpu.HBM)
     return pl.pallas_call(
@@ -486,7 +512,7 @@
         out_specs=pl.BlockSpec(memory_space=pltpu.VMEM),
         scratch_shapes=scratch,
         compiler_params=pltpu.CompilerParams(
-            collective_id=0, has_side_effects=True, vmem_limit_bytes=42 * 1024 * 1024
+            collective_id=0, has_side_effects=True, vmem_limit_bytes=56557568
         ),
     )(offsets, fraction, radial_diff, radial_drift, loop_diff, height_diff, fields)
 

time: 258 us -> 246 us (0.953)
  Pallas kernels: 246 us -> 240 us
  local copies, waits for them, and re-layouts: 8.02 us -> 4.09 us
    pallas_call x1, Pallas kernels: 246 us -> 240 us  [local(): pl.pallas_call(functools.partial(kernel, n, rows), out_shape=pltpu.VMEM(f...]
    unnamed x13 -> x1, local copies, waits for them, and re-layouts: 8.02 us -> 4.09 us
where the time goes in v3:
time: 246 us; the launch traced here: 244 us
  Pallas kernels  240 us (98%)
  local copies, waits for them, and re-layouts  4.09 us (2%)
    pallas_call x1, Pallas kernels, local(): pl.pallas_call(functools.partial(kernel, n, rows), out_shape=pltpu.VMEM(f...  240 us

profile of v3, /device:TPU:0, one launch (start us, length us, event | category | flops | bytes accessed | tf_op | source)
XLA Modules:
  0.0 244.1 jit_solution(11747944120884674464)
XLA Ops:
  0.0 240.0 %shard_map.73 = f32[5,16,64,512]{3,2,1,0:T(8,128)S(1)} custom-call(s32[16]{0:T(128)} %offs_in.1, f32[16]{0:T(128)} %frac_in.1, f32[16]{0:T(128)} %diff_in.1, f32[16]{0:T(128)} %drift_in.1, f32[16]{0:T(128)} %loop_in.1, f32[64]{0:T(128)} %rise_in.1, f32[5,16,64,512]{3,2,1,0:T(8,128)} %fields_ref.1), custom_call_target="tpu_custom_call" | custom-call | tf_op jit(solution)/shard_map/pallas_call | solution.py:508
  240.0 4.1 %copy.9 = f32[5,16,64,512]{3,2,1,0:T(8,128)} copy(f32[5,16,64,512]{3,2,1,0:T(8,128)S(1)} %shard_map.73) | data formatting | bytes 20971520

commit v4 on v3

--- a/solution.py
+++ b/solution.py
@@ -105,6 +105,14 @@
     def _():
         pl.semaphore_wait(barrier, n)
 
+    order = sorted(range(2, n), key=lambda d: (d % 2, -d)) + [1]
+
+    def partner(d):
+        bits = n.bit_length() - 1
+        return sum(
+            lax.rem(me // (1 << k) + ((d >> k) & 1), 2) * (1 << k) for k in range(bits)
+        )
+
     def radius(owner, ri):
         if ri == 1:
             return owner + half
@@ -116,7 +124,7 @@
         )
 
     def in_copy(f, ri, d):
-        to = lax.rem(me + d, n)
+        to = partner(d)
         return pltpu.make_async_remote_copy(
             src_ref=fields_ref.at[f, radius(to, ri)],
             dst_ref=loops.at[f, me, ri],
@@ -127,7 +135,7 @@
         )
 
     def back_copy(f, ri, d):
-        to = lax.rem(me + d, n)
+        to = partner(d)
         return pltpu.make_async_remote_copy(
             src_ref=stage.at[f, to, ri],
             dst_ref=state.at[f, HALO + radius(me, ri)],
@@ -138,7 +146,7 @@
         )
 
     def edge_copy(f, d):
-        to = lax.rem(me + d, n)
+        to = partner(d)
         return pltpu.make_async_remote_copy(
             src_ref=edge_stage.at[f, to],
             dst_ref=edges.at[f, me + HALO],
@@ -195,7 +203,7 @@
 
     for f in range(fields):
         for ri in range(per):
-            for d in range(1, n):
+            for d in order:
                 in_copy(f, ri, d).start()
             in_own(f, ri).start()
 
@@ -248,7 +256,7 @@
     def shift_field(f, carry):
         for ri in range(per):
             in_own(f, ri).wait()
-            for d in range(1, n):
+            for d in order:
                 in_copy(f, ri, d).wait_recv()
 
         def shift_loop(ri, carry):
@@ -308,11 +316,11 @@
 
         lax.fori_loop(0, n, pack_edges, 0)
         edge_own(f).start()
-        for d in range(1, n):
+        for d in order:
             edge_copy(f, d).start()
         for ri in range(per):
             back_own(f, ri).start()
-            for d in range(1, n):
+            for d in order:
                 back_copy(f, ri, d).start()
         return carry
 
@@ -345,7 +353,7 @@
     for f in range(fields):
         edge_own(f).wait()
         back_own(f, 0).wait()
-        for d in range(1, n):
+        for d in order:
             edge_copy(f, d).wait_recv()
             back_copy(f, 0, d).wait_recv()
 
@@ -437,13 +445,13 @@
         lax.fori_loop(1, half - 1, second, 0)
         lax.fori_loop(radii - half + 3, radii + 1, second, 0)
         back_own(f, 1).wait()
-        for d in range(1, n):
+        for d in order:
             back_copy(f, 1, d).wait_recv()
         lax.fori_loop(half + 1, radii + 2 * HALO - 1 - half, first, 0)
         lax.fori_loop(half - 1, radii - half + 3, second, 0)
 
     for f in range(fields):
-        for d in range(1, n):
+        for d in order:
             edge_copy(f, d).wait_send()
             for ri in range(per):
                 in_copy(f, ri, d).wait_send()

time: 246 us -> 247 us (level)
  no operation moved by 1% of the time
where the time goes in v4:
time: 247 us
  Pallas kernels  242 us (98%)
  local copies, waits for them, and re-layouts  4.09 us (2%)
    pallas_call x1, Pallas kernels, local(): pl.pallas_call(functools.partial(kernel, n, rows), out_shape=pltpu.VMEM(f...  242 us

profile of v4, /device:TPU:0, one launch (start us, length us, event | category | flops | bytes accessed | tf_op | source)
XLA Modules:
  0.0 246.5 jit_solution(1542876635976649756)
XLA Ops:
  0.0 242.4 %shard_map.73 = f32[5,16,64,512]{3,2,1,0:T(8,128)S(1)} custom-call(s32[16]{0:T(128)} %offs_in.1, f32[16]{0:T(128)} %frac_in.1, f32[16]{0:T(128)} %diff_in.1, f32[16]{0:T(128)} %drift_in.1, f32[16]{0:T(128)} %loop_in.1, f32[64]{0:T(128)} %rise_in.1, f32[5,16,64,512]{3,2,1,0:T(8,128)} %fields_ref.1), custom_call_target="tpu_custom_call" | custom-call | tf_op jit(solution)/shard_map/pallas_call | solution.py:516
  242.4 4.1 %copy.9 = f32[5,16,64,512]{3,2,1,0:T(8,128)} copy(f32[5,16,64,512]{3,2,1,0:T(8,128)S(1)} %shard_map.73) | data formatting | bytes 20971520
